TPU v7x, 32 devices: a whole 2x2x4 slice. The times are simulated.
32 devices in a mesh: gx: 8 (over z, y), gy: 4 (over x, core).
Axes of the slice: x: 2, y: 2, z: 4, core: 2. Of those that a mesh axis runs over, the one named last changes fastest.
Arguments:
- right_side: float32 [64, 128, 128], P('gy', 'gx'), may hold values from -6 to 9
- diagonal: float32 [64, 128, 128], P('gy', 'gx'), may hold values from 0.02 to 0.5
- horizontal: float32 [64, 128, 128], P('gy', 'gx'), may hold values from 0.1 to 1
- vertical: float32 [128], replicated, may hold values from 0.2 to 2
- precond: float32 [2, 128, 128], replicated, may hold values from -4 to 4
- edge_rows: int32 [2, 64], replicated, may hold values from 0 to 63, as said below
Outputs:
- solution_field: float32 [64, 128, 128], P('gy', 'gx')
- residual: float32 [64, 128, 128], P('gy', 'gx')
- residual_sq: float32 [3], replicated
Inputs may be any that keep to these rules, and one draw needn't show every extreme that they name: Each row of edge_rows lists every number 0 to 63 exactly once.
All inputs are finite; a program needn't handle non-finite values.
Results may differ from a plain program's by a relative error of at most 0.00014.
Values sent between devices are 32-bit elements; how exact they have to be, the bound alone decides.
No kernel may reach another device: no remote copies, remote signals or barrier semaphores. Data moves between devices by JAX's collectives and lax.ppermute only.
A program may use at most 64 MiB of HBM per device.

v0:
```python
import jax
import jax.numpy as jnp
from jax import lax
from jax.sharding import PartitionSpec as P

ITERS = 3


def padded(x, sides, width, wrap):
    for axis, dim in sides:
        devices, length = (lax.axis_size(axis), x.shape[dim])
        up = [(i, (i + 1) % devices) for i in range(devices if wrap else devices - 1)]
        down = [(j, i) for i, j in up]
        last = lax.slice_in_dim(x, length - width, length, axis=dim)
        initial = lax.slice_in_dim(x, 0, width, axis=dim)
        before = lax.ppermute(last, axis, up)
        after = lax.ppermute(initial, axis, down)
        x = jnp.concatenate([before, x, after], axis=dim)
    return x


def local_product(left, right):
    return jnp.sum(left * right)


def on_device(right_side, diagonal, horizontal, vertical, precond, edge_rows):
    rows, cols, levels = right_side.shape
    n_gx = lax.axis_size("gx")
    n_gy = lax.axis_size("gy")
    col_index = lax.axis_index("gx")
    row_index = lax.axis_index("gy")
    total_cells = float(rows * cols * levels * n_gx * n_gy)
    half = n_gx // 2
    panel = (col_index >= half).astype(jnp.int32)
    matrix = lax.dynamic_index_in_dim(precond, panel, 0, keepdims=False)
    east_table = jnp.where(col_index == half - 1, edge_rows[0], edge_rows[1])
    west_table = jnp.where(col_index == half, edge_rows[0], edge_rows[1])
    first_row = row_index * rows
    east_local = lax.dynamic_slice_in_dim(east_table, first_row, rows)
    west_local = lax.dynamic_slice_in_dim(west_table, first_row, rows)
    east_border = (col_index == half - 1) | (col_index == n_gx - 1)
    west_border = (col_index == half) | (col_index == 0)
    solution_field = jnp.zeros_like(right_side)
    residual = right_side
    directions = []
    images = []
    norms = []
    for step in range(ITERS):
        pre = jnp.einsum("yxl,kl->yxk", residual, matrix, precision=lax.Precision.HIGHEST)
        wide = padded(pre, (("gx", 1),), 1, True)
        edges = jnp.stack([wide[:, 0], wide[:, -1]], 0)
        whole = lax.all_gather(edges, "gy", axis=1, tiled=True)
        west_fix = jnp.take(whole[0], west_local, axis=0)
        east_fix = jnp.take(whole[1], east_local, axis=0)
        west = jnp.where(west_border, west_fix, edges[0])
        east = jnp.where(east_border, east_fix, edges[1])
        tall = padded(pre, (("gy", 0),), 1, False)
        flat = jnp.pad(pre, ((0, 0), (0, 0), (1, 1)))
        east_side = jnp.concatenate([pre[:, 1:], east[:, None]], 1)
        west_side = jnp.concatenate([west[:, None], pre[:, :-1]], 1)
        beside = east_side + west_side + tall[2:] + tall[:-2]
        column = flat[:, :, 2:] + flat[:, :, :-2]
        image = diagonal * pre + horizontal * (4.0 * pre - beside) + vertical * (2.0 * pre - column)
        count = len(images)
        terms = [local_product(image, older) for older in images]
        terms = terms + [local_product(residual, older) for older in images]
        terms = terms + [local_product(image, image), local_product(residual, image)]
        if step > 0:
            terms.append(local_product(residual, residual))
        totals = lax.psum(jnp.stack(terms), ("gx", "gy")) / total_cells
        coeffs = totals[:count]
        against = totals[count : 2 * count]
        square = totals[2 * count] - jnp.sum(coeffs * coeffs)
        along = totals[2 * count + 1] - jnp.sum(coeffs * against)
        if step > 0:
            norms.append(totals[2 * count + 2])
        for number in range(count):
            pre = pre - coeffs[number] * directions[number]
            image = image - coeffs[number] * images[number]
        scale = 1.0 / jnp.sqrt(square)
        alpha = along * scale
        direction = pre * scale
        image = image * scale
        solution_field = solution_field + alpha * direction
        residual = residual - alpha * image
        directions.append(direction)
        images.append(image)
    norms.append(lax.psum(local_product(residual, residual), ("gx", "gy")) / total_cells)
    return (solution_field, residual, jnp.stack(norms))


def solution(mesh):
    in_specs = (P("gy", "gx", None), P("gy", "gx", None), P("gy", "gx", None), P(), P(), P())
    out_specs = (P("gy", "gx", None), P("gy", "gx", None), P())
    return jax.shard_map(
        on_device, mesh=mesh, in_specs=in_specs, out_specs=out_specs, check_vma=False
    )
```

profile of v0, /device:TPU:0, one launch (start us, length us, event | category | flops | bytes accessed | tf_op | source)
XLA Modules:
  0.0 243.0 jit_solution(2497374235617542815)
XLA Ops:
  2.7 1.3 collective-permute-start.2
  4.0 3.0 %collective-permute-start.3 = (f32[1,16,128]{2,1,0:T(8,128)S(1)}, f32[1,16,128]{2,1,0:T(8,128)S(1)}, u32[]{:S(2)}, u32[]{:S(2)}) collective-permute-start(f32[1,16,128]{2,1,0:T(8,128)S(1)} %get-tuple-element.48), channel_id=1, source_target_pairs={{0,1},{1,2},{2,3},{4,5},{5,6},{6,7},{8,9},{9,10},{10,11},{12,13},{... | collective-permute-start | bytes 24584 | tf_op jit(solution)/shard_map/ppermute | solution.py:16
  7.1 3.0 %collective-permute-start = (f32[16,1,128]{2,0,1:T(8,128)S(1)}, f32[16,1,128]{2,0,1:T(8,128)S(1)}, u32[]{:S(2)}, u32[]{:S(2)}) collective-permute-start(f32[16,1,128]{2,0,1:T(8,128)S(1)} %bitcast.112), channel_id=1, source_target_pairs={{0,4},{4,8},{8,12},{12,16},{16,20},{20,24},{24,28},{28,0},{1,5},{5... | collective-permute-start | bytes 24584 | tf_op jit(solution)/shard_map/ppermute | solution.py:16
  10.1 3.1 %collective-permute-start.1 = (f32[16,1,128]{2,0,1:T(8,128)S(1)}, f32[16,1,128]{2,0,1:T(8,128)S(1)}, u32[]{:S(2)}, u32[]{:S(2)}) collective-permute-start(f32[16,1,128]{2,0,1:T(8,128)S(1)} %bitcast.111), channel_id=1, source_target_pairs={{4,0},{8,4},{12,8},{16,12},{20,16},{24,20},{28,24},{0,28},{5,1},{9... | collective-permute-start | bytes 24584 | tf_op jit(solution)/shard_map/ppermute | solution.py:17
  14.8 5.4 %all_gather.9 = f32[2,64,128]{2,1,0:T(8,128)S(1)} all-gather(f32[2,16,128]{2,1,0:T(8,128)S(1)} %pad_maximum_fusion.6), channel_id=1, replica_groups=mesh['gx'=8,'gy'=4] {'gy'}, dimensions={1}, use_global_device_ids=true | all-gather | bytes 81920 | tf_op jit(solution)/shard_map/all_gather | solution.py:52
  22.9 1.4 pad_maximum_fusion.9
  24.3 40.2 %psum.28 = f32[2]{0:T(128)S(1)} all-reduce(f32[2]{0:T(128)S(1)} %pad_maximum_fusion.9), channel_id=1, replica_groups=mesh['gx'=8,'gy'=4] {'gx','gy'}, use_global_device_ids=true, to_apply=%region_2.4 | all-reduce | flops 2 | bytes 16 | tf_op jit(solution)/shard_map/psum | solution.py:70
  66.8 2.3 collective-permute-start.4
  69.1 2.5 %collective-permute-start.5 = (f32[16,1,128]{2,0,1:T(8,128)S(1)}, f32[16,1,128]{2,0,1:T(8,128)S(1)}, u32[]{:S(2)}, u32[]{:S(2)}) collective-permute-start(f32[16,1,128]{2,0,1:T(8,128)S(1)} %bitcast.113), channel_id=1, source_target_pairs={{4,0},{8,4},{12,8},{16,12},{20,16},{24,20},{28,24},{0,28},{5,1},{9... | collective-permute-start | bytes 24584 | tf_op jit(solution)/shard_map/ppermute | solution.py:17
  71.6 1.3 collective-permute-start.6
  72.9 3.0 %collective-permute-start.7 = (f32[1,16,128]{2,1,0:T(8,128)S(1)}, f32[1,16,128]{2,1,0:T(8,128)S(1)}, u32[]{:S(2)}, u32[]{:S(2)}) collective-permute-start(f32[1,16,128]{2,1,0:T(8,128)S(1)} %get-tuple-element.42), channel_id=1, source_target_pairs={{0,1},{1,2},{2,3},{4,5},{5,6},{6,7},{8,9},{9,10},{10,11},{12,13},{... | collective-permute-start | bytes 24584 | tf_op jit(solution)/shard_map/ppermute | solution.py:16
  75.9 5.8 %all_gather.10 = f32[2,64,128]{2,1,0:T(8,128)S(1)} all-gather(f32[2,16,128]{2,1,0:T(8,128)S(1)} %pad_maximum_fusion.7), channel_id=1, replica_groups=mesh['gx'=8,'gy'=4] {'gy'}, dimensions={1}, use_global_device_ids=true | all-gather | bytes 81920 | tf_op jit(solution)/shard_map/all_gather | solution.py:52
  83.8 3.2 %stack.76 = f32[5]{0:T(128)S(1)} concatenate(f32[1]{0:T(128)} %bitcast.28, f32[1]{0:T(128)} %bitcast.29, f32[1]{0:T(128)} %bitcast.30, f32[1]{0:T(128)} %bitcast.31, f32[1]{0:T(128)} %bitcast.32), dimensions={0} | concatenate | bytes 40 | tf_op jit(solution)/shard_map/stack | solution.py:70
  87.1 37.9 %psum.29 = f32[5]{0:T(128)S(1)} all-reduce(f32[5]{0:T(128)S(1)} %stack.76), channel_id=1, replica_groups=mesh['gx'=8,'gy'=4] {'gx','gy'}, use_global_device_ids=true, to_apply=%region_8.10 | all-reduce | flops 5 | bytes 40 | tf_op jit(solution)/shard_map/psum | solution.py:70
  130.4 2.3 collective-permute-start.8
  132.7 2.5 %collective-permute-start.9 = (f32[16,1,128]{2,0,1:T(8,128)S(1)}, f32[16,1,128]{2,0,1:T(8,128)S(1)}, u32[]{:S(2)}, u32[]{:S(2)}) collective-permute-start(f32[16,1,128]{2,0,1:T(8,128)S(1)} %bitcast.114), channel_id=1, source_target_pairs={{4,0},{8,4},{12,8},{16,12},{20,16},{24,20},{28,24},{0,28},{5,1},{9... | collective-permute-start | bytes 24584 | tf_op jit(solution)/shard_map/ppermute | solution.py:17
  136.5 3.0 %collective-permute-start.11 = (f32[1,16,128]{2,1,0:T(8,128)S(1)}, f32[1,16,128]{2,1,0:T(8,128)S(1)}, u32[]{:S(2)}, u32[]{:S(2)}) collective-permute-start(f32[1,16,128]{2,1,0:T(8,128)S(1)} %get-tuple-element.36), channel_id=1, source_target_pairs={{0,1},{1,2},{2,3},{4,5},{5,6},{6,7},{8,9},{9,10},{10,11},{12,13},{... | collective-permute-start | bytes 24584 | tf_op jit(solution)/shard_map/ppermute | solution.py:16
  139.6 5.8 %all_gather.11 = f32[2,64,128]{2,1,0:T(8,128)S(1)} all-gather(f32[2,16,128]{2,1,0:T(8,128)S(1)} %pad_maximum_fusion.8), channel_id=1, replica_groups=mesh['gx'=8,'gy'=4] {'gy'}, dimensions={1}, use_global_device_ids=true | all-gather | bytes 81920 | tf_op jit(solution)/shard_map/all_gather | solution.py:52
  147.5 4.5 %stack.85 = f32[7]{0:T(128)S(1)} concatenate(f32[1]{0:T(128)} %bitcast.46, f32[1]{0:T(128)} %bitcast.47, f32[1]{0:T(128)} %bitcast.48, f32[1]{0:T(128)} %bitcast.49, f32[1]{0:T(128)} %bitcast.50, f32[1]{0:T(128)} %bitcast.51, f32[1]{0:T(128)} %bitcast.52), dimensions={0} | concatenate | bytes 56 | tf_op jit(solution)/shard_map/stack | solution.py:70
  152.0 38.1 %psum.30 = f32[7]{0:T(128)S(1)} all-reduce(f32[7]{0:T(128)S(1)} %stack.85), channel_id=1, replica_groups=mesh['gx'=8,'gy'=4] {'gx','gy'}, use_global_device_ids=true, to_apply=%region_16.18 | all-reduce | flops 7 | bytes 56 | tf_op jit(solution)/shard_map/psum | solution.py:70
  194.1 2.6 %multiply_add_fusion = f32[16,16,128]{2,1,0:T(8,128)} fusion(f32[16,16,128]{2,1,0:T(8,128)S(1)} %fusion.27, f32[16,16,128]{2,1,0:T(8,128)S(1)} %fusion.29, f32[16,16,128]{2,1,0:T(8,128)S(1)} %convolution_bitcast_fusion, f32[]{:T(128)S(6)} %sqrt.17, f32[]{:T(128)} %bitcast.56, f32[]{:T(128)} %bitcast.55, f32[]{:T(128)S(6)} %mul.267, f32[]{:T(128)} %bitcast.34, ...), kind=kLoop, calls=%fused_computation.51 | loop fusion | flops 458752 | bytes 524324 | tf_op jit(solution)/shard_map/add | solution.py:84
  196.7 2.5 %multiply_reduce_fusion = (f32[]{:T(128)}, f32[16,16,128]{2,1,0:T(8,128)}) fusion(f32[16,16,128]{2,1,0:T(8,128)S(1)} %get-tuple-element.23, f32[]{:T(128)S(6)} %sqrt.17, f32[16,16,128]{2,1,0:T(8,128)S(1)} %get-tuple-element.24, f32[]{:T(128)} %bitcast.56, f32[16,16,128]{2,1,0:T(8,128)S(1)} %get-tuple-element.22, f32[16,16,128]{2,1,0:T(8,128)S(1)} %get-tuple-element.26, ...), kind=kLoop, calls=%fused_computation.49 | loop fusion | flops 327679 | bytes 655384 | tf_op jit(solution)/shard_map/reduce_sum | solution.py:23
  199.2 41.3 %psum.31 = f32[]{:T(128)} all-reduce(f32[]{:T(128)} %get-tuple-element.20), channel_id=1, replica_groups=mesh['gx'=8,'gy'=4] {'gx','gy'}, use_global_device_ids=true, to_apply=%region_20.22 | all-reduce | flops 1 | bytes 8 | tf_op jit(solution)/shard_map/psum | solution.py:88
  241.2 1.8 pad_maximum_fusion.10
  (72 shorter events, 15.7 us)
Async XLA Ops:
  0.6 0.9 copy-start
  2.7 18.8 %collective-permute-start.2 = (f32[1,16,128]{2,1,0:T(8,128)S(1)}, f32[1,16,128]{2,1,0:T(8,128)S(1)}, u32[]{:S(2)}, u32[]{:S(2)}) collective-permute-start(f32[1,16,128]{2,1,0:T(8,128)S(1)} %get-tuple-element.47), channel_id=1, source_target_pairs={{1,0},{2,1},{3,2},{5,4},{6,5},{7,6},{9,8},{10,9},{11,10},{13,12},{... | collective-permute-start | bytes 24584 | tf_op jit(solution)/shard_map/ppermute | solution.py:17
  4.0 17.5 %collective-permute-start.3 = (f32[1,16,128]{2,1,0:T(8,128)S(1)}, f32[1,16,128]{2,1,0:T(8,128)S(1)}, u32[]{:S(2)}, u32[]{:S(2)}) collective-permute-start(f32[1,16,128]{2,1,0:T(8,128)S(1)} %get-tuple-element.48), channel_id=1, source_target_pairs={{0,1},{1,2},{2,3},{4,5},{5,6},{6,7},{8,9},{9,10},{10,11},{12,13},{... | collective-permute-start | bytes 24584 | tf_op jit(solution)/shard_map/ppermute | solution.py:16
  7.1 7.7 %collective-permute-start = (f32[16,1,128]{2,0,1:T(8,128)S(1)}, f32[16,1,128]{2,0,1:T(8,128)S(1)}, u32[]{:S(2)}, u32[]{:S(2)}) collective-permute-start(f32[16,1,128]{2,0,1:T(8,128)S(1)} %bitcast.112), channel_id=1, source_target_pairs={{0,4},{4,8},{8,12},{12,16},{16,20},{20,24},{24,28},{28,0},{1,5},{5... | collective-permute-start | bytes 24584 | tf_op jit(solution)/shard_map/ppermute | solution.py:16
  10.1 4.7 %collective-permute-start.1 = (f32[16,1,128]{2,0,1:T(8,128)S(1)}, f32[16,1,128]{2,0,1:T(8,128)S(1)}, u32[]{:S(2)}, u32[]{:S(2)}) collective-permute-start(f32[16,1,128]{2,0,1:T(8,128)S(1)} %bitcast.111), channel_id=1, source_target_pairs={{4,0},{8,4},{12,8},{16,12},{20,16},{24,20},{28,24},{0,28},{5,1},{9... | collective-permute-start | bytes 24584 | tf_op jit(solution)/shard_map/ppermute | solution.py:17
  13.3 0.7 copy-start.5
  14.8 6.7 %copy-start.3 = (f32[16,16,128]{2,1,0:T(8,128)S(1)}, f32[16,16,128]{2,1,0:T(8,128)}, u32[]{:S(2)}) copy-start(f32[16,16,128]{2,1,0:T(8,128)} %param.9) | copy-start | bytes 393220
  20.2 1.3 copy-start.2
  20.2 1.3 copy-start.1
  21.5 0.7 copy-start.4
  66.8 9.1 %collective-permute-start.4 = (f32[16,1,128]{2,0,1:T(8,128)S(1)}, f32[16,1,128]{2,0,1:T(8,128)S(1)}, u32[]{:S(2)}, u32[]{:S(2)}) collective-permute-start(f32[16,1,128]{2,0,1:T(8,128)S(1)} %bitcast.115), channel_id=1, source_target_pairs={{0,4},{4,8},{8,12},{12,16},{16,20},{20,24},{24,28},{28,0},{1,5},{5... | collective-permute-start | bytes 24584 | tf_op jit(solution)/shard_map/ppermute | solution.py:16
  69.1 6.8 %collective-permute-start.5 = (f32[16,1,128]{2,0,1:T(8,128)S(1)}, f32[16,1,128]{2,0,1:T(8,128)S(1)}, u32[]{:S(2)}, u32[]{:S(2)}) collective-permute-start(f32[16,1,128]{2,0,1:T(8,128)S(1)} %bitcast.113), channel_id=1, source_target_pairs={{4,0},{8,4},{12,8},{16,12},{20,16},{24,20},{28,24},{0,28},{5,1},{9... | collective-permute-start | bytes 24584 | tf_op jit(solution)/shard_map/ppermute | solution.py:17
  71.6 11.5 %collective-permute-start.6 = (f32[1,16,128]{2,1,0:T(8,128)S(1)}, f32[1,16,128]{2,1,0:T(8,128)S(1)}, u32[]{:S(2)}, u32[]{:S(2)}) collective-permute-start(f32[1,16,128]{2,1,0:T(8,128)S(1)} %get-tuple-element.41), channel_id=1, source_target_pairs={{1,0},{2,1},{3,2},{5,4},{6,5},{7,6},{9,8},{10,9},{11,10},{13,12},{... | collective-permute-start | bytes 24584 | tf_op jit(solution)/shard_map/ppermute | solution.py:17
  72.9 10.2 %collective-permute-start.7 = (f32[1,16,128]{2,1,0:T(8,128)S(1)}, f32[1,16,128]{2,1,0:T(8,128)S(1)}, u32[]{:S(2)}, u32[]{:S(2)}) collective-permute-start(f32[1,16,128]{2,1,0:T(8,128)S(1)} %get-tuple-element.42), channel_id=1, source_target_pairs={{0,1},{1,2},{2,3},{4,5},{5,6},{6,7},{8,9},{9,10},{10,11},{12,13},{... | collective-permute-start | bytes 24584 | tf_op jit(solution)/shard_map/ppermute | solution.py:16
  130.4 9.1 %collective-permute-start.8 = (f32[16,1,128]{2,0,1:T(8,128)S(1)}, f32[16,1,128]{2,0,1:T(8,128)S(1)}, u32[]{:S(2)}, u32[]{:S(2)}) collective-permute-start(f32[16,1,128]{2,0,1:T(8,128)S(1)} %bitcast.116), channel_id=1, source_target_pairs={{0,4},{4,8},{8,12},{12,16},{16,20},{20,24},{24,28},{28,0},{1,5},{5... | collective-permute-start | bytes 24584 | tf_op jit(solution)/shard_map/ppermute | solution.py:16
  132.7 6.8 %collective-permute-start.9 = (f32[16,1,128]{2,0,1:T(8,128)S(1)}, f32[16,1,128]{2,0,1:T(8,128)S(1)}, u32[]{:S(2)}, u32[]{:S(2)}) collective-permute-start(f32[16,1,128]{2,0,1:T(8,128)S(1)} %bitcast.114), channel_id=1, source_target_pairs={{4,0},{8,4},{12,8},{16,12},{20,16},{24,20},{28,24},{0,28},{5,1},{9... | collective-permute-start | bytes 24584 | tf_op jit(solution)/shard_map/ppermute | solution.py:17
  135.2 11.5 %collective-permute-start.10 = (f32[1,16,128]{2,1,0:T(8,128)S(1)}, f32[1,16,128]{2,1,0:T(8,128)S(1)}, u32[]{:S(2)}, u32[]{:S(2)}) collective-permute-start(f32[1,16,128]{2,1,0:T(8,128)S(1)} %get-tuple-element.35), channel_id=1, source_target_pairs={{1,0},{2,1},{3,2},{5,4},{6,5},{7,6},{9,8},{10,9},{11,10},{13,12},{... | collective-permute-start | bytes 24584 | tf_op jit(solution)/shard_map/ppermute | solution.py:17
  136.5 10.2 %collective-permute-start.11 = (f32[1,16,128]{2,1,0:T(8,128)S(1)}, f32[1,16,128]{2,1,0:T(8,128)S(1)}, u32[]{:S(2)}, u32[]{:S(2)}) collective-permute-start(f32[1,16,128]{2,1,0:T(8,128)S(1)} %get-tuple-element.36), channel_id=1, source_target_pairs={{0,1},{1,2},{2,3},{4,5},{5,6},{6,7},{8,9},{9,10},{10,11},{12,13},{... | collective-permute-start | bytes 24584 | tf_op jit(solution)/shard_map/ppermute | solution.py:16
where the time goes:
time: 244 us; the launch traced here: 243 us
  blocking collectives  175 us (72%)
  starting transfers between devices  28.6 us (12%)
  local copies, waits for them, and re-layouts  15.2 us (6%)
  other arithmetic  12.7 us (5%)
  between operations  9.45 us (4%)
    psum x3, blocking collectives, on_device(): totals = lax.psum(jnp.stack(terms), ('gx', 'gy')) / total_cells  116 us
    psum x1, blocking collectives, on_device(): lax.psum(local_product(residual, residual), ('gx', 'gy')) / total_cells  41.3 us
    all_gather x3, blocking collectives, on_device(): whole = lax.all_gather(edges, 'gy', axis=1, tiled=True)  17 us
    ppermute x6, starting transfers between devices, padded(): before = lax.ppermute(last, axis, up)  16.8 us
    ppermute x6, starting transfers between devices, padded(): after = lax.ppermute(initial, axis, down)  11.9 us
    another operation x2, local copies, waits for them, and re-layouts, on_device(): totals = lax.psum(jnp.stack(terms), ('gx', 'gy')) / total_cells  7.69 us
    reduce_sum x4, other arithmetic, local_product(): return jnp.sum(left * right)  4.94 us
  transfers between devices with their start and end apart: 12, of which 1 were waited for; matrix products, arithmetic and copies ran while one was open for 2% of the time, Pallas kernels for 0%

commit v1 on v0

--- a/solution.py
+++ b/solution.py
@@ -1,9 +1,18 @@
+import functools
 import jax
 import jax.numpy as jnp
 from jax import lax
 from jax.sharding import PartitionSpec as P
 
 ITERS = 3
+
+
+def _take_column(view, chip_axis):
+    next_value = lax.all_gather(view, axis_name=chip_axis)
+    return jnp.sum(next_value, axis=0)
+
+
+do_the_view = functools.partial(_take_column, chip_axis=("gx", "gy"))
 
 
 def padded(x, sides, width, wrap):
@@ -67,7 +76,7 @@
         terms = terms + [local_product(image, image), local_product(residual, image)]
         if step > 0:
             terms.append(local_product(residual, residual))
-        totals = lax.psum(jnp.stack(terms), ("gx", "gy")) / total_cells
+        totals = do_the_view(jnp.stack(terms)) / total_cells
         coeffs = totals[:count]
         against = totals[count : 2 * count]
         square = totals[2 * count] - jnp.sum(coeffs * coeffs)

time: 244 us -> 242 us (level)
  blocking collectives: 175 us -> 172 us
    psum x3 -> x0, blocking collectives: 116 us -> none  [on_device(): totals = lax.psum(jnp.stack(terms), ('gx', 'gy')) / total_cells]
    unnamed x0 -> x3, blocking collectives: none -> 114 us
  transfers between devices with their start and end apart: 12 -> 12, of which waited for: 1 -> 0; matrix products, arithmetic and copies ran while one was open for 2% -> 2% of each run, Pallas kernels for 0% -> 0%
where the time goes in v1:
time: 242 us; the launch traced here: 241 us
  blocking collectives  172 us (71%)
  starting transfers between devices  28.6 us (12%)
  local copies, waits for them, and re-layouts  15.9 us (7%)
  other arithmetic  12.9 us (5%)
  between operations  9.51 us (4%)
    unnamed x3, blocking collectives  114 us
    psum x1, blocking collectives, on_device(): lax.psum(local_product(residual, residual), ('gx', 'gy')) / total_cells  41.5 us
    all_gather x3, blocking collectives, on_device(): whole = lax.all_gather(edges, 'gy', axis=1, tiled=True)  17 us
    ppermute x6, starting transfers between devices, padded(): before = lax.ppermute(last, axis, up)  16.8 us
    ppermute x6, starting transfers between devices, padded(): after = lax.ppermute(initial, axis, down)  11.9 us
    another operation x2, local copies, waits for them, and re-layouts, on_device(): totals = do_the_view(jnp.stack(terms)) / total_cells  7.69 us
    reduce_sum x4, other arithmetic, local_product(): return jnp.sum(left * right)  4.94 us
  transfers between devices with their start and end apart: 12, of which 0 were waited for; matrix products, arithmetic and copies ran while one was open for 2% of the time, Pallas kernels for 0%

profile of v1, /device:TPU:0, one launch (start us, length us, event | category | flops | bytes accessed | tf_op | source)
XLA Modules:
  0.0 241.1 jit_solution(4157309998689740637)
XLA Ops:
  2.7 3.0 %collective-permute-start = (f32[16,1,128]{2,0,1:T(8,128)S(1)}, f32[16,1,128]{2,0,1:T(8,128)S(1)}, u32[]{:S(2)}, u32[]{:S(2)}) collective-permute-start(f32[16,1,128]{2,0,1:T(8,128)S(1)} %bitcast.112), channel_id=1, source_target_pairs={{0,4},{4,8},{8,12},{12,16},{16,20},{20,24},{24,28},{28,0},{1,5},{5... | collective-permute-start | bytes 24584 | tf_op jit(solution)/shard_map/ppermute | solution.py:25
  5.8 3.1 %collective-permute-start.1 = (f32[16,1,128]{2,0,1:T(8,128)S(1)}, f32[16,1,128]{2,0,1:T(8,128)S(1)}, u32[]{:S(2)}, u32[]{:S(2)}) collective-permute-start(f32[16,1,128]{2,0,1:T(8,128)S(1)} %bitcast.111), channel_id=1, source_target_pairs={{4,0},{8,4},{12,8},{16,12},{20,16},{24,20},{28,24},{0,28},{5,1},{9... | collective-permute-start | bytes 24584 | tf_op jit(solution)/shard_map/ppermute | solution.py:26
  8.9 1.3 collective-permute-start.2
  10.2 3.0 %collective-permute-start.3 = (f32[1,16,128]{2,1,0:T(8,128)S(1)}, f32[1,16,128]{2,1,0:T(8,128)S(1)}, u32[]{:S(2)}, u32[]{:S(2)}) collective-permute-start(f32[1,16,128]{2,1,0:T(8,128)S(1)} %get-tuple-element.48), channel_id=1, source_target_pairs={{0,1},{1,2},{2,3},{4,5},{5,6},{6,7},{8,9},{9,10},{10,11},{12,13},{... | collective-permute-start | bytes 24584 | tf_op jit(solution)/shard_map/ppermute | solution.py:25
  14.2 5.4 %all_gather.27 = f32[2,64,128]{2,1,0:T(8,128)S(1)} all-gather(f32[2,16,128]{2,1,0:T(8,128)S(1)} %pad_maximum_fusion.6), channel_id=1, replica_groups=mesh['gx'=8,'gy'=4] {'gy'}, dimensions={1}, use_global_device_ids=true | all-gather | bytes 81920 | tf_op jit(solution)/shard_map/all_gather | solution.py:61
  22.3 1.5 maximum_dynamic-update-slice_fusion
  23.8 37.8 %all-reduce.3 = f32[64]{0:T(128)S(1)} all-reduce(f32[64]{0:T(128)S(1)} %maximum_dynamic-update-slice_fusion), channel_id=2, replica_groups=mesh['gx'=8,'gy'=4] {'gx','gy'}, use_global_device_ids=true, to_apply=%add.3 | all-reduce | flops 64 | bytes 512
  64.0 2.3 collective-permute-start.4
  66.3 2.5 %collective-permute-start.5 = (f32[16,1,128]{2,0,1:T(8,128)S(1)}, f32[16,1,128]{2,0,1:T(8,128)S(1)}, u32[]{:S(2)}, u32[]{:S(2)}) collective-permute-start(f32[16,1,128]{2,0,1:T(8,128)S(1)} %bitcast.113), channel_id=1, source_target_pairs={{4,0},{8,4},{12,8},{16,12},{20,16},{24,20},{28,24},{0,28},{5,1},{9... | collective-permute-start | bytes 24584 | tf_op jit(solution)/shard_map/ppermute | solution.py:26
  68.8 1.3 collective-permute-start.6
  70.1 3.0 %collective-permute-start.7 = (f32[1,16,128]{2,1,0:T(8,128)S(1)}, f32[1,16,128]{2,1,0:T(8,128)S(1)}, u32[]{:S(2)}, u32[]{:S(2)}) collective-permute-start(f32[1,16,128]{2,1,0:T(8,128)S(1)} %get-tuple-element.42), channel_id=1, source_target_pairs={{0,1},{1,2},{2,3},{4,5},{5,6},{6,7},{8,9},{9,10},{10,11},{12,13},{... | collective-permute-start | bytes 24584 | tf_op jit(solution)/shard_map/ppermute | solution.py:25
  73.2 5.8 %all_gather.30 = f32[2,64,128]{2,1,0:T(8,128)S(1)} all-gather(f32[2,16,128]{2,1,0:T(8,128)S(1)} %pad_maximum_fusion.7), channel_id=1, replica_groups=mesh['gx'=8,'gy'=4] {'gy'}, dimensions={1}, use_global_device_ids=true | all-gather | bytes 81920 | tf_op jit(solution)/shard_map/all_gather | solution.py:61
  81.1 3.2 %stack.76 = f32[5]{0:T(128)S(1)} concatenate(f32[1]{0:T(128)} %bitcast.28, f32[1]{0:T(128)} %bitcast.29, f32[1]{0:T(128)} %bitcast.30, f32[1]{0:T(128)} %bitcast.31, f32[1]{0:T(128)} %bitcast.32), dimensions={0} | concatenate | bytes 40 | tf_op jit(solution)/shard_map/stack | solution.py:79
  84.5 38.0 %all-reduce.4 = f32[160]{0:T(256)S(1)} all-reduce(f32[160]{0:T(256)S(1)} %dynamic-update-slice.1), channel_id=3, replica_groups=mesh['gx'=8,'gy'=4] {'gx','gy'}, use_global_device_ids=true, to_apply=%add.4 | all-reduce | flops 160 | bytes 1280
  128.1 2.3 collective-permute-start.8
  130.4 2.5 %collective-permute-start.9 = (f32[16,1,128]{2,0,1:T(8,128)S(1)}, f32[16,1,128]{2,0,1:T(8,128)S(1)}, u32[]{:S(2)}, u32[]{:S(2)}) collective-permute-start(f32[16,1,128]{2,0,1:T(8,128)S(1)} %bitcast.114), channel_id=1, source_target_pairs={{4,0},{8,4},{12,8},{16,12},{20,16},{24,20},{28,24},{0,28},{5,1},{9... | collective-permute-start | bytes 24584 | tf_op jit(solution)/shard_map/ppermute | solution.py:26
  134.2 3.0 %collective-permute-start.11 = (f32[1,16,128]{2,1,0:T(8,128)S(1)}, f32[1,16,128]{2,1,0:T(8,128)S(1)}, u32[]{:S(2)}, u32[]{:S(2)}) collective-permute-start(f32[1,16,128]{2,1,0:T(8,128)S(1)} %get-tuple-element.36), channel_id=1, source_target_pairs={{0,1},{1,2},{2,3},{4,5},{5,6},{6,7},{8,9},{9,10},{10,11},{12,13},{... | collective-permute-start | bytes 24584 | tf_op jit(solution)/shard_map/ppermute | solution.py:25
  137.3 5.8 %all_gather.33 = f32[2,64,128]{2,1,0:T(8,128)S(1)} all-gather(f32[2,16,128]{2,1,0:T(8,128)S(1)} %pad_maximum_fusion.8), channel_id=1, replica_groups=mesh['gx'=8,'gy'=4] {'gy'}, dimensions={1}, use_global_device_ids=true | all-gather | bytes 81920 | tf_op jit(solution)/shard_map/all_gather | solution.py:61
  145.2 4.5 %stack.85 = f32[7]{0:T(128)S(1)} concatenate(f32[1]{0:T(128)} %bitcast.46, f32[1]{0:T(128)} %bitcast.47, f32[1]{0:T(128)} %bitcast.48, f32[1]{0:T(128)} %bitcast.49, f32[1]{0:T(128)} %bitcast.50, f32[1]{0:T(128)} %bitcast.51, f32[1]{0:T(128)} %bitcast.52), dimensions={0} | concatenate | bytes 56 | tf_op jit(solution)/shard_map/stack | solution.py:79
  149.9 38.0 %all-reduce.5 = f32[224]{0:T(256)S(1)} all-reduce(f32[224]{0:T(256)S(1)} %dynamic-update-slice.2), channel_id=4, replica_groups=mesh['gx'=8,'gy'=4] {'gx','gy'}, use_global_device_ids=true, to_apply=%add.5 | all-reduce | flops 224 | bytes 1792
  192.1 2.6 %multiply_add_fusion = f32[16,16,128]{2,1,0:T(8,128)} fusion(f32[16,16,128]{2,1,0:T(8,128)S(1)} %fusion.27, f32[16,16,128]{2,1,0:T(8,128)S(1)} %fusion.29, f32[16,16,128]{2,1,0:T(8,128)S(1)} %convolution_bitcast_fusion, f32[]{:T(128)S(6)} %sqrt.17, f32[]{:T(128)} %bitcast.56, f32[]{:T(128)} %bitcast.55, f32[]{:T(128)S(6)} %mul.267, f32[]{:T(128)} %bitcast.34, ...), kind=kLoop, calls=%fused_computation.51 | loop fusion | flops 458752 | bytes 524324 | tf_op jit(solution)/shard_map/add | solution.py:93
  194.6 2.5 %multiply_reduce_fusion = (f32[]{:T(128)}, f32[16,16,128]{2,1,0:T(8,128)}) fusion(f32[16,16,128]{2,1,0:T(8,128)S(1)} %get-tuple-element.23, f32[]{:T(128)S(6)} %sqrt.17, f32[16,16,128]{2,1,0:T(8,128)S(1)} %get-tuple-element.24, f32[]{:T(128)} %bitcast.56, f32[16,16,128]{2,1,0:T(8,128)S(1)} %get-tuple-element.22, f32[16,16,128]{2,1,0:T(8,128)S(1)} %get-tuple-element.26, ...), kind=kLoop, calls=%fused_computation.49 | loop fusion | flops 327679 | bytes 655384 | tf_op jit(solution)/shard_map/reduce_sum | solution.py:32
  197.2 41.5 %psum.7 = f32[]{:T(128)} all-reduce(f32[]{:T(128)} %get-tuple-element.20), channel_id=1, replica_groups=mesh['gx'=8,'gy'=4] {'gx','gy'}, use_global_device_ids=true, to_apply=%region_20.22 | all-reduce | flops 1 | bytes 8 | tf_op jit(solution)/shard_map/psum | solution.py:97
  239.3 1.8 pad_maximum_fusion.9
  (83 shorter events, 15.9 us)
Async XLA Ops:
  0.6 0.9 copy-start
  2.7 11.4 %collective-permute-start = (f32[16,1,128]{2,0,1:T(8,128)S(1)}, f32[16,1,128]{2,0,1:T(8,128)S(1)}, u32[]{:S(2)}, u32[]{:S(2)}) collective-permute-start(f32[16,1,128]{2,0,1:T(8,128)S(1)} %bitcast.112), channel_id=1, source_target_pairs={{0,4},{4,8},{8,12},{12,16},{16,20},{20,24},{24,28},{28,0},{1,5},{5... | collective-permute-start | bytes 24584 | tf_op jit(solution)/shard_map/ppermute | solution.py:25
  5.8 8.4 %collective-permute-start.1 = (f32[16,1,128]{2,0,1:T(8,128)S(1)}, f32[16,1,128]{2,0,1:T(8,128)S(1)}, u32[]{:S(2)}, u32[]{:S(2)}) collective-permute-start(f32[16,1,128]{2,0,1:T(8,128)S(1)} %bitcast.111), channel_id=1, source_target_pairs={{4,0},{8,4},{12,8},{16,12},{20,16},{24,20},{28,24},{0,28},{5,1},{9... | collective-permute-start | bytes 24584 | tf_op jit(solution)/shard_map/ppermute | solution.py:26
  8.9 12.0 %collective-permute-start.2 = (f32[1,16,128]{2,1,0:T(8,128)S(1)}, f32[1,16,128]{2,1,0:T(8,128)S(1)}, u32[]{:S(2)}, u32[]{:S(2)}) collective-permute-start(f32[1,16,128]{2,1,0:T(8,128)S(1)} %get-tuple-element.47), channel_id=1, source_target_pairs={{1,0},{2,1},{3,2},{5,4},{6,5},{7,6},{9,8},{10,9},{11,10},{13,12},{... | collective-permute-start | bytes 24584 | tf_op jit(solution)/shard_map/ppermute | solution.py:26
  10.2 10.7 %collective-permute-start.3 = (f32[1,16,128]{2,1,0:T(8,128)S(1)}, f32[1,16,128]{2,1,0:T(8,128)S(1)}, u32[]{:S(2)}, u32[]{:S(2)}) collective-permute-start(f32[1,16,128]{2,1,0:T(8,128)S(1)} %get-tuple-element.48), channel_id=1, source_target_pairs={{0,1},{1,2},{2,3},{4,5},{5,6},{6,7},{8,9},{9,10},{10,11},{12,13},{... | collective-permute-start | bytes 24584 | tf_op jit(solution)/shard_map/ppermute | solution.py:25
  13.3 0.7 copy-start.5
  14.2 6.7 %copy-start.3 = (f32[16,16,128]{2,1,0:T(8,128)S(1)}, f32[16,16,128]{2,1,0:T(8,128)}, u32[]{:S(2)}) copy-start(f32[16,16,128]{2,1,0:T(8,128)} %param.9) | copy-start | bytes 393220
  19.6 1.3 copy-start.2
  19.6 1.3 copy-start.1
  20.9 0.7 copy-start.4
  64.0 9.1 %collective-permute-start.4 = (f32[16,1,128]{2,0,1:T(8,128)S(1)}, f32[16,1,128]{2,0,1:T(8,128)S(1)}, u32[]{:S(2)}, u32[]{:S(2)}) collective-permute-start(f32[16,1,128]{2,0,1:T(8,128)S(1)} %bitcast.115), channel_id=1, source_target_pairs={{0,4},{4,8},{8,12},{12,16},{16,20},{20,24},{24,28},{28,0},{1,5},{5... | collective-permute-start | bytes 24584 | tf_op jit(solution)/shard_map/ppermute | solution.py:25
  66.3 6.8 %collective-permute-start.5 = (f32[16,1,128]{2,0,1:T(8,128)S(1)}, f32[16,1,128]{2,0,1:T(8,128)S(1)}, u32[]{:S(2)}, u32[]{:S(2)}) collective-permute-start(f32[16,1,128]{2,0,1:T(8,128)S(1)} %bitcast.113), channel_id=1, source_target_pairs={{4,0},{8,4},{12,8},{16,12},{20,16},{24,20},{28,24},{0,28},{5,1},{9... | collective-permute-start | bytes 24584 | tf_op jit(solution)/shard_map/ppermute | solution.py:26
  68.8 11.5 %collective-permute-start.6 = (f32[1,16,128]{2,1,0:T(8,128)S(1)}, f32[1,16,128]{2,1,0:T(8,128)S(1)}, u32[]{:S(2)}, u32[]{:S(2)}) collective-permute-start(f32[1,16,128]{2,1,0:T(8,128)S(1)} %get-tuple-element.41), channel_id=1, source_target_pairs={{1,0},{2,1},{3,2},{5,4},{6,5},{7,6},{9,8},{10,9},{11,10},{13,12},{... | collective-permute-start | bytes 24584 | tf_op jit(solution)/shard_map/ppermute | solution.py:26
  70.1 10.2 %collective-permute-start.7 = (f32[1,16,128]{2,1,0:T(8,128)S(1)}, f32[1,16,128]{2,1,0:T(8,128)S(1)}, u32[]{:S(2)}, u32[]{:S(2)}) collective-permute-start(f32[1,16,128]{2,1,0:T(8,128)S(1)} %get-tuple-element.42), channel_id=1, source_target_pairs={{0,1},{1,2},{2,3},{4,5},{5,6},{6,7},{8,9},{9,10},{10,11},{12,13},{... | collective-permute-start | bytes 24584 | tf_op jit(solution)/shard_map/ppermute | solution.py:25
  128.1 9.1 %collective-permute-start.8 = (f32[16,1,128]{2,0,1:T(8,128)S(1)}, f32[16,1,128]{2,0,1:T(8,128)S(1)}, u32[]{:S(2)}, u32[]{:S(2)}) collective-permute-start(f32[16,1,128]{2,0,1:T(8,128)S(1)} %bitcast.116), channel_id=1, source_target_pairs={{0,4},{4,8},{8,12},{12,16},{16,20},{20,24},{24,28},{28,0},{1,5},{5... | collective-permute-start | bytes 24584 | tf_op jit(solution)/shard_map/ppermute | solution.py:25
  130.4 6.8 %collective-permute-start.9 = (f32[16,1,128]{2,0,1:T(8,128)S(1)}, f32[16,1,128]{2,0,1:T(8,128)S(1)}, u32[]{:S(2)}, u32[]{:S(2)}) collective-permute-start(f32[16,1,128]{2,0,1:T(8,128)S(1)} %bitcast.114), channel_id=1, source_target_pairs={{4,0},{8,4},{12,8},{16,12},{20,16},{24,20},{28,24},{0,28},{5,1},{9... | collective-permute-start | bytes 24584 | tf_op jit(solution)/shard_map/ppermute | solution.py:26
  132.9 11.5 %collective-permute-start.10 = (f32[1,16,128]{2,1,0:T(8,128)S(1)}, f32[1,16,128]{2,1,0:T(8,128)S(1)}, u32[]{:S(2)}, u32[]{:S(2)}) collective-permute-start(f32[1,16,128]{2,1,0:T(8,128)S(1)} %get-tuple-element.35), channel_id=1, source_target_pairs={{1,0},{2,1},{3,2},{5,4},{6,5},{7,6},{9,8},{10,9},{11,10},{13,12},{... | collective-permute-start | bytes 24584 | tf_op jit(solution)/shard_map/ppermute | solution.py:26
  134.2 10.2 %collective-permute-start.11 = (f32[1,16,128]{2,1,0:T(8,128)S(1)}, f32[1,16,128]{2,1,0:T(8,128)S(1)}, u32[]{:S(2)}, u32[]{:S(2)}) collective-permute-start(f32[1,16,128]{2,1,0:T(8,128)S(1)} %get-tuple-element.36), channel_id=1, source_target_pairs={{0,1},{1,2},{2,3},{4,5},{5,6},{6,7},{8,9},{9,10},{10,11},{12,13},{... | collective-permute-start | bytes 24584 | tf_op jit(solution)/shard_map/ppermute | solution.py:25
